TPU v7x, 256 devices: a whole 4x4x8 slice. The times are simulated.
256 devices in a mesh: grp: 32 (over z, x_lo, core), freq: 8 (over x_hi, y).
Axes of the slice: x: 4 (x_hi: 2, x_lo: 2; x = x_hi * 2 + x_lo), y: 4, z: 8, core: 2. Of those that a mesh axis runs over, the one named last changes fastest.
Arguments:
- spectra: bfloat16 [8, 8192, 1024], P('freq', 'grp'), may hold values from -3000 to 3000
- valid: int32 [8192, 512], P('grp'), may hold values 0 or 1
- station_index: int32 [16], replicated, may hold values from 0 to 8191, as said below
Outputs:
- cross: bfloat16 [8, 2, 8192, 8192], P('freq', None, 'grp')
- station_gather: float32 [16, 8192, 256], P(None, 'grp', 'freq')
Inputs may be any that keep to these rules, and one draw needn't show every extreme that they name: `station_index`: 16 distinct channel numbers.
All inputs are finite; a program needn't handle non-finite values. No bound on the sum of `valid` on one device may be relied on, other than what follows from the above.
Results may differ from a plain program's by a relative error of at most 0.0056.
Values may be sent and summed in bfloat16 or wider, within the bound.
A program may use at most 128 MiB of HBM per device.

v0:
```python
import math
import jax
import jax.numpy as jnp
from jax import lax
from jax.sharding import Mesh
from jax.sharding import PartitionSpec as P

LAGS = 256
GRP = ("chip", "core")


def on_device(spectra, valid, station_index):
    bin_count, chan_count, double_width = spectra.shape
    window_count = double_width // 2
    spectrum_f32 = spectra.astype(jnp.float32)
    real_part = spectrum_f32[..., :window_count]
    imag_part = spectrum_f32[..., window_count:]
    local_power = jnp.sum(real_part * real_part + imag_part * imag_part, axis=0)
    band_power = lax.psum(local_power, "freq")
    freq_count = lax.axis_size("freq")
    total_bins = bin_count * freq_count
    factor = lax.rsqrt(band_power / total_bins + 1e-05) * valid.astype(jnp.float32)
    whitened = (spectrum_f32 * jnp.concatenate([factor, factor], axis=1)[None]).astype(jnp.bfloat16)
    swapped = jnp.concatenate([whitened[..., window_count:], -whitened[..., :window_count]], axis=2)
    stacked = jnp.concatenate([whitened, swapped], axis=1)
    scaling = 1.0 / math.sqrt(window_count)
    chip_count = lax.axis_size("chip")
    core_count = lax.axis_size("core")
    same_core = lax.all_gather(whitened, "chip", axis=1)
    both_cores = lax.all_gather(same_core, "core", axis=2)
    peer_rows = both_cores.reshape(bin_count, chip_count * core_count * chan_count, double_width)
    product = jnp.einsum("bkw,bjw->bkj", stacked, peer_rows, preferred_element_type=jnp.float32)
    cross = (
        (product * scaling)
        .astype(jnp.bfloat16)
        .reshape(bin_count, 2, chan_count, peer_rows.shape[1])
    )
    station_count = station_index.shape[0]
    station_rows = jnp.take(peer_rows, station_index, axis=1)
    station_swapped = jnp.concatenate(
        [station_rows[..., window_count:], -station_rows[..., :window_count]], axis=2
    )
    station_left = jnp.concatenate([station_rows, station_swapped], axis=1)
    kernel = (
        jnp.einsum("bkw,bjw->bkj", station_left, whitened, preferred_element_type=jnp.float32)
        * scaling
    )
    kernel = kernel.reshape(bin_count, 2, station_count, chan_count)
    all_bins = lax.all_gather(kernel, "freq", axis=0, tiled=True)
    lag_share = LAGS // freq_count
    freq_index = lax.axis_index("freq")
    bin_values = jnp.arange(total_bins, dtype=jnp.float32) + 1.0
    lag_values = (freq_index * lag_share + jnp.arange(lag_share, dtype=jnp.int32)).astype(
        jnp.float32
    )
    phase = math.pi * bin_values[:, None] * lag_values[None, :] / LAGS
    lag_table = jnp.stack([jnp.cos(phase), -jnp.sin(phase)], axis=1)
    station_gather = jnp.einsum(
        "frsc,frl->scl", all_bins, lag_table, precision=lax.Precision.HIGHEST
    ) / math.sqrt(total_bins)
    return (cross, station_gather)


def solution(mesh):
    grp_size, freq_size = mesh.devices.shape
    fine = Mesh(mesh.devices.reshape(grp_size // 2, 2, freq_size), ("chip", "core", "freq"))
    placed = (P("freq", GRP, None), P(GRP, None), P())
    return jax.shard_map(
        on_device,
        mesh=fine,
        in_specs=placed,
        out_specs=(P("freq", None, GRP, None), P(None, GRP, "freq")),
        check_vma=False,
    )
```

profile of v0, /device:TPU:8, one launch (start us, length us, event | category | flops | bytes accessed | tf_op | source)
XLA Modules:
  0.0 394.3 jit_solution(18342799320419296325)
XLA Ops:
  7.2 0.0 all-reduce.2.cloned.1.call-start
  7.2 1.1 convert_element_type.20
  8.4 0.9 fusion.8
  9.3 0.0 all-reduce.2.cloned.1.call-update
  9.3 0.0 all-gather.5.cloned.1.call-start
  9.3 91.7 %all-reduce.2.cloned.1.call-done = f32[256,512]{1,0:T(8,128)} async-done(((f32[256,512]{1,0:T(8,128)}), f32[256,512]{1,0:T(8,128)}) %all-reduce.2.cloned.1.call-update) | async-done | bytes 524304 | tf_op jit(solution)/shard_map/psum | solution.py:19
  101.1 1.3 convert_multiply_fusion
  102.4 2.0 fusion.2
  104.3 0.0 all-gather.5.cloned.1.call-update
  104.4 0.0 all-gather.7.cloned.1.call-start
  104.4 184.2 %all-gather.5.cloned.1.call-done = bf16[16,256,1024]{2,1,0:T(8,128)(2,1)} async-done(((bf16[1,256,1024]{2,1,0:T(8,128)(2,1)}), bf16[16,256,1024]{2,1,0:T(8,128)(2,1)}) %all-gather.5.cloned.1.call-update) | async-done | bytes 8388624 | tf_op jit(solution)/shard_map/all_gather | solution.py:29
  288.6 0.0 all-gather.7.cloned.1.call-update
  288.7 0.7 compare_select_fusion
  289.3 0.7 compare_and_fusion
  290.0 0.1 fusion.17
  290.1 1.1 fusion.21
  291.2 36.0 %all-gather.7.cloned.1.call-done = bf16[16,512,1024]{2,1,0:T(8,128)(2,1)} async-done(((bf16[16,256,1024]{2,1,0:T(8,128)(2,1)}), bf16[16,512,1024]{2,1,0:T(8,128)(2,1)}) %all-gather.7.cloned.1.call-update) | async-done | bytes 16777232 | tf_op jit(solution)/shard_map/all_gather | solution.py:30
  327.2 8.5 %gather_fusion = bf16[16,1024]{1,0:T(8,128)(2,1)S(1)} fusion(bf16[8192,1024]{1,0:T(8,128)(2,1)} %bitcast.32, s32[1024]{0:T(1024)S(1)} %pad_clamp_fusion), kind=kCustom, calls=%fused_computation | custom fusion | bytes 65600 | tf_op jit(solution)/shard_map/jit(_take)/gather | solution.py:39
  335.7 0.1 bitcast_select_fusion
  335.8 1.3 convolution_multiply_fusion
  337.1 34.6 %all_gather.19 = f32[8,2,16,256]{3,2,1,0:T(8,128)S(1)} all-gather(f32[1,2,16,256]{3,2,1,0:T(8,128)S(1)} %bitcast.31), channel_id=1, replica_groups=mesh['chip'=16,'core'=2,'freq'=8] {'freq'}, dimensions={0}, use_global_device_ids=true | all-gather | bytes 294912 | tf_op jit(solution)/shard_map/all_gather | solution.py:49
  371.7 14.5 %multiply_convert_fusion = bf16[512,8192]{1,0:T(8,128)(2,1)} fusion(bf16[8192,1024]{1,0:T(8,128)(2,1)} %bitcast.33, bf16[1,256,512]{2,1,0:T(8,128)(2,1)S(1)} %get-tuple-element.3, bf16[1,256,512]{2,1,0:T(8,128)(2,1)S(1)} %get-tuple-element.2, bf16[1,256,1024]{2,1,0:T(8,128)(2,1)} %fusion.2), kind=kOutput, calls=%fused_computation.1 | convolution fusion | flops 8601468928 | bytes 26214400 | tf_op jit(solution)/shard_map/bkw,bjw->bkj/dot_general | solution.py:32
  386.3 1.5 fusion
  (4 shorter events, 0.0 us)
Async XLA Ops:
  7.2 93.9 %all-reduce.2.cloned.1.call-start = ((), (), s32[]{:S(2)}) async-start(), calls=%async_computation | async-start | bytes 1048576 | tf_op jit(solution)/shard_map/psum | solution.py:19
  9.3 279.3 %all-gather.5.cloned.1.call-start = ((), (), s32[]{:S(2)}) async-start(), calls=%async_computation.1 | async-start | bytes 8912896 | tf_op jit(solution)/shard_map/all_gather | solution.py:29
  104.4 222.8 %all-gather.7.cloned.1.call-start = ((), (), s32[]{:S(2)}) async-start(), calls=%async_computation.2 | async-start | bytes 25165824 | tf_op jit(solution)/shard_map/all_gather | solution.py:30
Sparse Core Ops, SparseCore 0:
  11.2 89.8 all-reduce.1
  104.5 184.0 all-gather.4
  290.6 36.5 all-gather.6
where the time goes:
time: 395 us; the launch traced here: 394 us
  waiting for transfers between devices  312 us (79%)
  blocking collectives  34.6 us (9%)
  matrix products  17.3 us (4%)
  between operations  13.8 us (3%)
  local copies, waits for them, and re-layouts  8.53 us (2%)
  other arithmetic  7.93 us (2%)
    all_gather x1, waiting for transfers between devices, on_device(): same_core = lax.all_gather(whitened, 'chip', axis=1)  184 us
    psum x1, waiting for transfers between devices, on_device(): band_power = lax.psum(local_power, 'freq')  91.7 us
    all_gather x1, waiting for transfers between devices, on_device(): both_cores = lax.all_gather(same_core, 'core', axis=2)  36 us
    all_gather x1, blocking collectives, on_device(): all_bins = lax.all_gather(kernel, 'freq', axis=0, tiled=True)  34.6 us
    dot_general x1, matrix products, on_device(): jnp.einsum('bkw,bjw->bkj', stacked, peer_rows, preferred_element_type=jnp...  14.5 us
    gather x1, local copies, waits for them, and re-layouts, on_device(): station_rows = jnp.take(peer_rows, station_index, axis=1)  8.53 us
  transfers between devices with their start and end apart: 3, of which 3 were waited for; matrix products, arithmetic and copies ran while one was open for 1% of the time, Pallas kernels for 0%

commit v1 on v0

--- a/solution.py
+++ b/solution.py
@@ -46,7 +46,9 @@
         * scaling
     )
     kernel = kernel.reshape(bin_count, 2, station_count, chan_count)
-    all_bins = lax.all_gather(kernel, "freq", axis=0, tiled=True)
+    all_bins = jnp.concatenate(
+        lax.all_to_all(jnp.stack([kernel] * lax.axis_size("freq")), "freq", 0, 0), axis=0
+    )
     lag_share = LAGS // freq_count
     freq_index = lax.axis_index("freq")
     bin_values = jnp.arange(total_bins, dtype=jnp.float32) + 1.0

time: 395 us -> 369 us (0.934)
  blocking collectives: 34.6 us -> 0 us
  starting transfers between devices: 0.12 us -> 7.36 us
    all_gather x1 -> x0, blocking collectives: 34.6 us -> none  [on_device(): all_bins = lax.all_gather(kernel, 'freq', axis=0, tiled=True)]
    all_to_all x0 -> x1, starting transfers between devices: none -> 7.24 us  [on_device(): lax.all_to_all(jnp.stack([kernel] * lax.axis_size('freq')), 'freq', 0, 0)]
  transfers between devices with their start and end apart: 3 -> 4, of which waited for: 3 -> 3; matrix products, arithmetic and copies ran while one was open for 1% -> 5% of each run, Pallas kernels for 0% -> 0%
where the time goes in v1:
time: 369 us; the launch traced here: 368 us
  waiting for transfers between devices  312 us (85%)
  matrix products  17.3 us (5%)
  between operations  13.8 us (4%)
  local copies, waits for them, and re-layouts  9.34 us (3%)
  other arithmetic  7.93 us (2%)
  starting transfers between devices  7.36 us (2%)
    all_gather x1, waiting for transfers between devices, on_device(): same_core = lax.all_gather(whitened, 'chip', axis=1)  184 us
    psum x1, waiting for transfers between devices, on_device(): band_power = lax.psum(local_power, 'freq')  91.7 us
    all_gather x1, waiting for transfers between devices, on_device(): both_cores = lax.all_gather(same_core, 'core', axis=2)  36 us
    dot_general x1, matrix products, on_device(): jnp.einsum('bkw,bjw->bkj', stacked, peer_rows, preferred_element_type=jnp...  14.5 us
    gather x1, local copies, waits for them, and re-layouts, on_device(): station_rows = jnp.take(peer_rows, station_index, axis=1)  8.53 us
  transfers between devices with their start and end apart: 4, of which 3 were waited for; matrix products, arithmetic and copies ran while one was open for 5% of the time, Pallas kernels for 0%

profile of v1, /device:TPU:8, one launch (start us, length us, event | category | flops | bytes accessed | tf_op | source)
XLA Modules:
  0.0 367.7 jit_solution(8293517150846007481)
XLA Ops:
  7.2 0.0 all-reduce.2.cloned.1.call-start
  7.2 1.1 convert_element_type.20
  8.4 0.9 fusion.8
  9.3 0.0 all-reduce.2.cloned.1.call-update
  9.3 0.0 all-gather.5.cloned.1.call-start
  9.3 91.7 %all-reduce.2.cloned.1.call-done = f32[256,512]{1,0:T(8,128)} async-done(((f32[256,512]{1,0:T(8,128)}), f32[256,512]{1,0:T(8,128)}) %all-reduce.2.cloned.1.call-update) | async-done | bytes 524304 | tf_op jit(solution)/shard_map/psum | solution.py:19
  101.1 1.3 convert_multiply_fusion
  102.4 2.0 fusion.2
  104.3 0.0 all-gather.5.cloned.1.call-update
  104.4 0.0 all-gather.7.cloned.1.call-start
  104.4 184.2 %all-gather.5.cloned.1.call-done = bf16[16,256,1024]{2,1,0:T(8,128)(2,1)} async-done(((bf16[1,256,1024]{2,1,0:T(8,128)(2,1)}), bf16[16,256,1024]{2,1,0:T(8,128)(2,1)}) %all-gather.5.cloned.1.call-update) | async-done | bytes 8388624 | tf_op jit(solution)/shard_map/all_gather | solution.py:29
  288.6 0.0 all-gather.7.cloned.1.call-update
  288.7 0.7 compare_select_fusion
  289.3 0.7 compare_and_fusion
  290.0 0.1 fusion.18
  290.1 1.1 fusion.22
  291.2 36.0 %all-gather.7.cloned.1.call-done = bf16[16,512,1024]{2,1,0:T(8,128)(2,1)} async-done(((bf16[16,256,1024]{2,1,0:T(8,128)(2,1)}), bf16[16,512,1024]{2,1,0:T(8,128)(2,1)}) %all-gather.7.cloned.1.call-update) | async-done | bytes 16777232 | tf_op jit(solution)/shard_map/all_gather | solution.py:30
  327.2 8.5 %gather_fusion = bf16[16,1024]{1,0:T(8,128)(2,1)S(1)} fusion(bf16[8192,1024]{1,0:T(8,128)(2,1)} %bitcast.35, s32[1024]{0:T(1024)S(1)} %pad_clamp_fusion), kind=kCustom, calls=%fused_computation | custom fusion | bytes 65600 | tf_op jit(solution)/shard_map/jit(_take)/gather | solution.py:39
  335.7 0.1 bitcast_select_fusion
  335.8 1.3 convolution_multiply_fusion
  337.1 0.8 stack.8
  337.9 7.2 %all-to-all-start = ((f32[8,1,2,16,256]{4,2,3,1,0:T(2,128)}), f32[8,1,2,16,256]{4,2,3,1,0:T(2,128)S(1)}, u32[]{:S(2)}, u32[]{:S(2)}) async-start(f32[8,1,2,16,256]{4,2,3,1,0:T(2,128)} %stack.8), calls=%async_computation | async-start | bytes 524288 | tf_op jit(solution)/shard_map/all_to_all | solution.py:50
  345.2 14.5 %multiply_convert_fusion = bf16[512,8192]{1,0:T(8,128)(2,1)} fusion(bf16[8192,1024]{1,0:T(8,128)(2,1)} %bitcast.36, bf16[1,256,512]{2,1,0:T(8,128)(2,1)S(1)} %get-tuple-element.3, bf16[1,256,512]{2,1,0:T(8,128)(2,1)S(1)} %get-tuple-element.2, bf16[1,256,1024]{2,1,0:T(8,128)(2,1)} %fusion.2), kind=kOutput, calls=%fused_computation.1 | convolution fusion | flops 8601468928 | bytes 26214400 | tf_op jit(solution)/shard_map/bkw,bjw->bkj/dot_general | solution.py:32
  359.7 0.0 all-to-all-done
  359.7 1.5 fusion
  (5 shorter events, 0.1 us)
Async XLA Ops:
  7.2 93.9 %all-reduce.2.cloned.1.call-start = ((), (), s32[]{:S(2)}) async-start(), calls=%async_computation.1 | async-start | bytes 1048576 | tf_op jit(solution)/shard_map/psum | solution.py:19
  9.3 279.3 %all-gather.5.cloned.1.call-start = ((), (), s32[]{:S(2)}) async-start(), calls=%async_computation.2 | async-start | bytes 8912896 | tf_op jit(solution)/shard_map/all_gather | solution.py:29
  104.4 222.8 %all-gather.7.cloned.1.call-start = ((), (), s32[]{:S(2)}) async-start(), calls=%async_computation.3 | async-start | bytes 25165824 | tf_op jit(solution)/shard_map/all_gather | solution.py:30
  337.9 21.8 %all-to-all-start = ((f32[8,1,2,16,256]{4,2,3,1,0:T(2,128)}), f32[8,1,2,16,256]{4,2,3,1,0:T(2,128)S(1)}, u32[]{:S(2)}, u32[]{:S(2)}) async-start(f32[8,1,2,16,256]{4,2,3,1,0:T(2,128)} %stack.8), calls=%async_computation | async-start | bytes 524288 | tf_op jit(solution)/shard_map/all_to_all | solution.py:50
Sparse Core Ops, SparseCore 0:
  11.2 89.8 all-reduce.1
  104.5 184.0 all-gather.4
  290.6 36.5 all-gather.6
